TPU v7x, 128 devices: a whole 4x4x4 slice. The times are simulated.
128 devices in a mesh: layer: 4 (over y_lo, core), shard: 32 (over z, y_hi, x).
Axes of the slice: x: 4, y: 4 (y_hi: 2, y_lo: 2; y = y_hi * 2 + y_lo), z: 4, core: 2. Of those that a mesh axis runs over, the one named last changes fastest.
Arguments:
- input_acts: bfloat16 [8, 16384, 5120], P('layer', 'shard'), may hold values from -6 to 6
- output_grads: bfloat16 [8, 16384, 1024], P('layer', 'shard'), may hold values from -6 to 6
- input_inverse: bfloat16 [8, 5120, 5120], P('layer', 'shard'), may hold values from -1 to 2, as said below
- output_inverse: bfloat16 [8, 1024, 1024], P('layer', 'shard'), may hold values from -1 to 2, as said below
- query_input: bfloat16 [8, 5120, 512], P(None, 'shard'), may hold values from -0.0048828125 to 0.0048828125
- query_output: bfloat16 [8, 1024, 512], P(None, 'shard'), may hold values from -0.1875 to 0.1875
- layer_order: int32 [8], replicated, may hold values from 0 to 7, each once
Outputs:
- scores: float32 [16384, 16], P('shard', 'layer')
Inputs may be any that keep to these rules, and one draw needn't show every extreme that they name: `input_inverse`: symmetric in its last two dimensions, with a unit-sized diagonal. `output_inverse`: symmetric in its last two dimensions, with a unit-sized diagonal.
All inputs are finite; a program needn't handle non-finite values.
Results may differ from a plain program's by a relative error of at most 0.0045.
Values may be sent and summed in bfloat16 or wider, within the bound.
A program may use at most 128 MiB of HBM per device.

v0:
```python
import jax
import jax.numpy as jnp
from jax import lax
from jax.sharding import PartitionSpec as P

QUERIES = 16


def joined_along(tiles, dim):
    dims = list(tiles.shape[1:])
    dims[dim] *= tiles.shape[0]
    return jnp.moveaxis(tiles, 0, dim).reshape(dims)


def sent_to_all(shard, axis):
    devices = lax.axis_size(axis)
    return lax.all_to_all(
        jnp.broadcast_to(shard[None], (devices, *shard.shape)), axis, 0, 0, tiled=True
    )


def gather_directly(shard, axis, dim):
    return joined_along(sent_to_all(shard, axis), dim)


def shards(
    input_acts, output_grads, input_inverse, output_inverse, query_input, query_output, layer_order
):
    depth = input_acts.shape[0]
    tokens = input_acts.shape[1]
    first = lax.axis_index("layer") * depth
    chosen_in = []
    chosen_out = []
    for position in range(depth):
        model_layer = layer_order[first + position]
        chosen_in.append(lax.dynamic_index_in_dim(query_input, model_layer, 0, keepdims=False))
        chosen_out.append(lax.dynamic_index_in_dim(query_output, model_layer, 0, keepdims=False))
    vectors_in = jnp.stack(chosen_in, axis=1)
    vectors_out = jnp.stack(chosen_out, axis=1)
    width = vectors_in.shape[2]
    whole_in = lax.all_gather(vectors_in, "shard", axis=0, tiled=True)
    folded_in = jnp.einsum(
        "jsk,kjn->sjn", input_inverse, whole_in, preferred_element_type=jnp.float32
    ).astype(jnp.bfloat16)
    columns = input_acts
    left = jnp.einsum(
        "jti,ijn->jtn",
        columns,
        lax.all_gather(folded_in, "shard", axis=0, tiled=True),
        preferred_element_type=jnp.float32,
    )
    whole_out = gather_directly(vectors_out, "shard", 0)
    folded_out = jnp.einsum(
        "jsk,kjn->sjn", output_inverse, whole_out, preferred_element_type=jnp.float32
    ).astype(jnp.bfloat16)
    columns = output_grads
    right = jnp.einsum(
        "jti,ijn->jtn",
        columns,
        gather_directly(folded_out, "shard", 0),
        preferred_element_type=jnp.float32,
    )
    product = (left * right).reshape(depth, tokens, QUERIES, width // QUERIES).sum(axis=(0, 3))
    return lax.psum_scatter(product, "layer", scatter_dimension=1, tiled=True)


def solution(mesh):
    in_specs = (
        P("layer", "shard", None),
        P("layer", "shard", None),
        P("layer", "shard", None),
        P("layer", "shard", None),
        P(None, "shard", None),
        P(None, "shard", None),
        P(),
    )
    out_specs = P("shard", "layer")
    return jax.shard_map(shards, mesh=mesh, in_specs=in_specs, out_specs=out_specs, check_vma=False)
```

profile of v0, /device:TPU:1, one launch (start us, length us, event | category | flops | bytes accessed | tf_op | source)
XLA Modules:
  0.0 326.5 jit_solution(4169752645969869274)
XLA Ops:
  6.5 0.0 copy-start
  6.5 0.0 all-gather.3.cloned.1.call-start
  6.5 1.4 fusion.2
  11.6 1.0 dynamic-slice_bitcast_fusion.1
  12.6 0.8 pad_maximum_fusion
  13.4 0.0 all-gather.3.cloned.1.call-update
  13.4 0.0 all-gather.5.cloned.1.call-start
  13.4 119.2 %all-gather.3.cloned.1.call-done = bf16[5120,2,512]{2,0,1:T(8,128)(2,1)} async-done(((bf16[160,2,512]{2,0,1:T(8,128)(2,1)}), bf16[5120,2,512]{2,0,1:T(8,128)(2,1)}) %all-gather.3.cloned.1.call-update) | async-done | bytes 10485776 | tf_op jit(solution)/shard_map/all_gather | solution.py:41
  132.7 0.0 copy-done
  132.7 6.6 %fusion = bf16[160,2,512]{2,0,1:T(8,128)(2,1)} fusion(bf16[2,160,5120]{2,1,0:T(8,128)(2,1)S(1)} %copy-done, bf16[5120,2,512]{2,0,1:T(8,128)(2,1)} %all-gather.3.cloned.1.call-done), kind=kOutput, calls=%fused_computation.2 | convolution fusion | flops 1677885440 | bytes 14090240 | tf_op jit(solution)/shard_map/jsk,kjn->sjn/dot_general | solution.py:42
  139.2 0.0 all-gather.5.cloned.1.call-update
  139.3 0.8 dynamic-slice_bitcast_fusion.3
  140.1 0.2 broadcast_in_dim.4
  140.3 36.1 %all_to_all.10 = bf16[32,32,2,512]{3,1,2,0:T(8,128)(2,1)S(1)} all-to-all(bf16[32,32,2,512]{3,1,2,0:T(8,128)(2,1)S(1)} %broadcast_in_dim.4), channel_id=1, replica_groups=mesh['layer'=4,'shard'=32] {'shard'}, dimensions={0} | all-to-all | bytes 4194304 | tf_op jit(solution)/shard_map/all_to_all | solution.py:17
  176.4 0.0 copy-start.1
  176.5 0.2 copy.13
  176.7 0.7 copy-done.1
  177.4 0.4 fusion.1
  177.8 1.6 broadcast_in_dim.5
  179.4 0.0 copy-start.2
  179.4 5.1 %all-to-all-start.1 = ((bf16[32,32,2,512]{3,1,2,0:T(8,128)(2,1)}), bf16[32,32,2,512]{3,1,2,0:T(8,128)(2,1)}, u32[]{:S(2)}, u32[]{:S(2)}) async-start(bf16[32,32,2,512]{3,1,2,0:T(8,128)(2,1)} %broadcast_in_dim.5), calls=%async_computation.1 | async-start | bytes 4194304 | tf_op jit(solution)/shard_map/all_to_all | solution.py:17
  184.5 0.0 copy-done.2
  184.5 0.6 dynamic-slice
  185.7 34.5 %all-to-all-done.1 = bf16[32,32,2,512]{3,1,2,0:T(8,128)(2,1)} async-done(((bf16[32,32,2,512]{3,1,2,0:T(8,128)(2,1)}), bf16[32,32,2,512]{3,1,2,0:T(8,128)(2,1)}, u32[]{:S(2)}, u32[]{:S(2)}) %all-to-all-start.1) | async-done | bytes 2097184 | tf_op jit(solution)/shard_map/all_to_all | solution.py:17
  220.2 3.2 copy.14
  223.4 66.7 %all-gather.5.cloned.1.call-done = bf16[5120,2,512]{2,0,1:T(8,128)(2,1)} async-done(((bf16[160,2,512]{2,0,1:T(8,128)(2,1)}), bf16[5120,2,512]{2,0,1:T(8,128)(2,1)}) %all-gather.5.cloned.1.call-update) | async-done | bytes 10485776 | tf_op jit(solution)/shard_map/all_gather | solution.py:49
  290.1 13.7 %fusion.3 = f32[2,512,512]{2,1,0:T(8,128)} fusion(bf16[5120,2,512]{2,0,1:T(8,128)(2,1)} %all-gather.5.cloned.1.call-done, bf16[2,512,5120]{2,1,0:T(8,128)(2,1)} %param.7), kind=kOutput, calls=%fused_computation.14 | convolution fusion | flops 5368709120 | bytes 23068672 | tf_op jit(solution)/shard_map/jti,ijn->jtn/dot_general | solution.py:46
  303.7 4.6 %multiply_reduce_fusion = f32[512,512]{1,0:T(8,128)S(1)} fusion(f32[2,512,512]{2,1,0:T(8,128)} %fusion.3, bf16[1024,2,512]{2,0,1:T(8,128)(2,1)} %bitcast.29, bf16[2,512,1024]{2,1,0:T(8,128)(2,1)} %param.8), kind=kOutput, calls=%fused_computation | convolution fusion | flops 1074528256 | bytes 7340032 | tf_op jit(solution)/shard_map/jti,ijn->jtn/dot_general | solution.py:57
  308.3 0.2 bitcast_reduce_fusion
  308.5 10.6 %all-reduce = f32[512,16]{0,1:T(8,128)S(1)} all-reduce(f32[512,16]{0,1:T(8,128)S(1)} %bitcast_reduce_fusion), channel_id=2, replica_groups=mesh['layer'=4,'shard'=32] {'layer'}, use_global_device_ids=true, to_apply=%region_2.3.clone | all-reduce | flops 8192 | bytes 65536
  319.0 0.6 constant_dynamic-slice_fusion
  (1 shorter events, 0.0 us)
Async XLA Ops:
  6.5 126.1 %copy-start = (bf16[2,160,5120]{2,1,0:T(8,128)(2,1)S(1)}, bf16[2,160,5120]{2,1,0:T(8,128)(2,1)}, u32[]{:S(2)}) copy-start(bf16[2,160,5120]{2,1,0:T(8,128)(2,1)} %param.9) | copy-start | bytes 9830404
  6.5 126.1 %all-gather.3.cloned.1.call-start = ((), (), s32[]{:S(2)}) async-start(), calls=%async_computation.2 | async-start | bytes 10813440 | tf_op jit(solution)/shard_map/all_gather | solution.py:41
  13.4 276.7 %all-gather.5.cloned.1.call-start = ((), (), s32[]{:S(2)}) async-start(), calls=%async_computation.3 | async-start | bytes 10813440 | tf_op jit(solution)/shard_map/all_gather | solution.py:49
  176.4 0.9 copy-start.1
  179.4 5.1 %copy-start.2 = (u32[128]{0:T(128)S(1)}, u32[128]{0:T(128)}, u32[]{:S(2)}) copy-start(u32[128]{0:T(128)} %constant.36) | copy-start | bytes 1540
  179.4 40.8 %all-to-all-start.1 = ((bf16[32,32,2,512]{3,1,2,0:T(8,128)(2,1)}), bf16[32,32,2,512]{3,1,2,0:T(8,128)(2,1)}, u32[]{:S(2)}, u32[]{:S(2)}) async-start(bf16[32,32,2,512]{3,1,2,0:T(8,128)(2,1)} %broadcast_in_dim.5), calls=%async_computation.1 | async-start | bytes 4194304 | tf_op jit(solution)/shard_map/all_to_all | solution.py:17
Sparse Core Ops, SparseCore 0:
  13.5 119.1 all-gather.2
  139.4 150.6 all-gather.4
where the time goes:
time: 327 us; the launch traced here: 326 us
  waiting for transfers between devices  220 us (67%)
  blocking collectives  46.7 us (14%)
  matrix products  25.3 us (8%)
  between operations  17.7 us (5%)
  local copies, waits for them, and re-layouts  10.3 us (3%)
  starting transfers between devices  5.12 us (2%)
    all_gather x1, waiting for transfers between devices, shards(): whole_in = lax.all_gather(vectors_in, 'shard', axis=0, tiled=True)  119 us
    all_gather x1, waiting for transfers between devices, shards(): lax.all_gather(folded_in, 'shard', axis=0, tiled=True)  66.7 us
    all_to_all x1, blocking collectives, sent_to_all(): lax.all_to_all(jnp.broadcast_to(shard[None], (devices, *shard.shape)), ax...  36.1 us
    all_to_all x1, waiting for transfers between devices, sent_to_all(): lax.all_to_all(jnp.broadcast_to(shard[None], (devices, *shard.shape)), ax...  34.5 us
    dot_general x1, matrix products, shards(): jnp.einsum('jti,ijn->jtn', columns, lax.all_gather(folded_in, 'shard', ax...  13.7 us
    unnamed x1, blocking collectives  10.6 us
    dot_general x1, matrix products, shards(): jnp.einsum('jsk,kjn->sjn', input_inverse, whole_in, preferred_element_typ...  6.58 us
  transfers between devices with their start and end apart: 3, of which 3 were waited for; matrix products, arithmetic and copies ran while one was open for 2% of the time, Pallas kernels for 0%

commit v1 on v0

v1 whole, which is shorter than its diff:
```python
import functools

import jax
import jax.numpy as jnp
from jax import lax
from jax.experimental import pallas as pl
from jax.experimental.pallas import tpu as pltpu
from jax.sharding import PartitionSpec as P

MESH = pl.DeviceIdType.MESH
BF16 = jnp.bfloat16
F32 = jnp.float32

DIN = 5120
DOUT = 1024
WIDTH = 512
HALF = 256
SLOTS = 2
TOK = 512
RI = 160
RO = 32

JOBS = 12


def dot(a, b):
    return jnp.dot(a, b, preferred_element_type=F32)


def kernel(
    order, q_hbm, qo_hbm, a_hbm, g_hbm, h_hbm, ho_hbm, out,
    q_all, qo_all, qg, qog, hb, hob, part_s, part_r, parto_s, parto_r, own, owno,
    pre, preo, acts, grads, left, right, score, score_r,
    ss, rs, ls,
):
    group = lax.axis_index("layer")
    shard = lax.axis_index("shard")
    ylo, core = lax.div(group, 2), lax.rem(group, 2)
    z, yhi, x = lax.div(shard, 8), lax.rem(lax.div(shard, 4), 2), lax.rem(shard, 4)
    other = 1 - yhi

    def device(zz, yy, xx):
        return (group, zz * 8 + yy * 4 + xx)

    def turn(i, by):
        return lax.rem(i + by + 4, 4)

    near = {
        ("x", 1): device(z, yhi, turn(x, 1)),
        ("x", -1): device(z, yhi, turn(x, -1)),
        ("z", 1): device(turn(z, 1), yhi, x),
        ("z", -1): device(turn(z, -1), yhi, x),
    }
    across = device(z, other, x)
    mates = [
        (ylo * 2 + 1 - core, shard),
        ((1 - ylo) * 2 + core, shard),
        ((1 - ylo) * 2 + 1 - core, shard),
    ]
    sent = []
    ids = {}

    def sem(name):
        return ids.setdefault(name, len(ids))

    def send(name, src, dst, to):
        k = sem(name)
        copy = pltpu.make_async_remote_copy(
            src_ref=src, dst_ref=dst, send_sem=ss.at[k], recv_sem=rs.at[k],
            device_id=to, device_id_type=MESH,
        )
        copy.start()
        sent.append(copy)

    def recv(name, ref):
        k = sem(name)
        pltpu.make_async_remote_copy(
            src_ref=ref, dst_ref=ref, send_sem=ss.at[k], recv_sem=rs.at[k],
            device_id=across, device_id_type=MESH,
        ).wait_recv()

    local = {}

    def fetch(name, src, dst):
        copy = pltpu.make_async_copy(src, dst, ls.at[len(local)])
        copy.start()
        local[name] = copy

    def ready(name):
        local[name].wait()

    class Gather:
        def __init__(self, name, first, at, half):
            self.name, self.at, self.half = name, at, half
            self.first, self.second = first, "z" if first == "x" else "x"
            self.i, self.j = (x, z) if first == "x" else (z, x)

        def place(self, i, j):
            return self.at(j, i) if self.first == "x" else self.at(i, j)

        def block(self, i, part):
            return self.half(self.place(i, self.j), part)

        def line(self, j, part):
            return self.place(pl.ds(2 * part, 2), j)

        def key(self, *k):
            return (self.name, *k)

        def first_send(self):
            for by, parts in ((1, (0, 1)), (-1, (1, 0))):
                for part in parts:
                    ref = self.block(self.i, part)
                    send(self.key("a", by, part), ref, ref, near[self.first, by])

        def first_pass(self):
            for by, part in ((1, 0), (-1, 1)):
                ref = self.block(turn(self.i, -by), part)
                recv(self.key("a", by, part), ref)
                send(self.key("b", by), ref, ref, near[self.first, by])

        def first_end(self):
            for by, part in ((1, 1), (-1, 0)):
                recv(self.key("a", by, part), self.block(turn(self.i, -by), part))
            for by, part in ((1, 0), (-1, 1)):
                recv(self.key("b", by), self.block(turn(self.i, 2), part))

        def second_send(self):
            for by, parts in ((1, (0, 1)), (-1, (1, 0))):
                for part in parts:
                    ref = self.line(self.j, part)
                    send(self.key("c", by, part), ref, ref, near[self.second, by])

        def second_pass(self):
            for by, part in ((1, 0), (-1, 1)):
                ref = self.line(turn(self.j, -by), part)
                recv(self.key("c", by, part), ref)
                send(self.key("d", by), ref, ref, near[self.second, by])

        def second_end(self):
            for by, part in ((1, 1), (-1, 0)):
                recv(self.key("c", by, part), self.line(turn(self.j, -by), part))
            for by, part in ((1, 0), (-1, 1)):
                recv(self.key("d", by), self.line(turn(self.j, 2), part))

    rows = lambda ref, part: ref.at[..., pl.ds(RI // 2 * part, RI // 2), :]
    slots = lambda ref, part: ref.at[..., pl.ds(part, 1), :, :]
    axes = ("x", "z")

    def pair(make):
        return [make(h) for h in range(2)]

    def q_job(p):
        return pair(lambda h: Gather(("q", p, h), axes[h], lambda zz, xx: qg.at[p, h, zz, xx], rows))

    def p_job(p):
        return pair(lambda h: Gather(("p", p, h), axes[h], lambda zz, xx: pre.at[p, h, zz, :, xx], rows))

    qo_job = pair(lambda h: Gather(("qo", h), axes[h], lambda zz, xx: qog.at[h, zz, xx], slots))
    po_job = pair(lambda h: Gather(("po", h), axes[h], lambda zz, xx: preo.at[h, zz, :, xx], slots))
    q_jobs, p_jobs = [q_job(0), q_job(1)], [p_job(0), p_job(1)]

    def do(step, job):
        for gather in job:
            getattr(gather, step)()

    def columns(ref, p, zz, yy, width):
        return ref.at[p, :, pl.ds(pl.multiple_of((zz * 2 + yy) * width, width), width)]

    fetch("q", q_hbm, q_all)
    fetch("qo", qo_hbm, qo_all)
    barrier = pltpu.get_barrier_semaphore()
    peers = list(near.values()) + [across] + mates
    for peer in peers:
        pl.semaphore_signal(barrier, inc=1, device_id=peer, device_id_type=MESH)

    for p in range(SLOTS):
        for zz in range(4):
            fetch(("h", p, zz), columns(h_hbm, p, zz, yhi, 4 * RI), hb.at[p, zz, pl.ds(0, RI)])
            fetch(("ho", p, zz), columns(ho_hbm, p, zz, yhi, 4 * RO), hob.at[p, zz, pl.ds(0, RO)])

    def share_h(p, zz):
        send(("h", p, zz), columns(h_hbm, p, zz, other, 4 * RI), hb.at[p, zz, pl.ds(RI, RI)], across)

    def got_h(p):
        for zz in range(4):
            ready(("h", p, zz))
            recv(("h", p, zz), hb.at[p, zz, pl.ds(RI, RI)])

    ready("q")
    ready("qo")
    for p in range(SLOTS):
        m = order[group * SLOTS + p]
        for h in range(2):
            qg[p, h, z, x] = q_all[m, :, pl.ds(h * HALF, HALF)]
            qog[h, z, x, p] = qo_all[m, :, pl.ds(h * HALF, HALF)]

    pl.semaphore_wait(barrier, len(peers))
    do("first_send", q_jobs[0])
    for zz in range(4):
        share_h(0, zz)
    do("first_send", q_jobs[1])
    for p in range(SLOTS):
        for zz in range(4):
            fetch(("a", p, zz), a_hbm.at[p, :, pl.ds(zz * 8 * RI, 8 * RI)], acts.at[p, zz])
    fetch("g", g_hbm, grads)

    def share_part(p):
        got_h(p)
        for h in range(2):
            def add(zz, acc):
                return acc + dot(hb[p, zz], qg[p, h, zz].reshape(4 * RI, HALF))
            acc = lax.fori_loop(0, 4, add, jnp.zeros((2 * RI, HALF), F32))
            own[p, h] = acc[:RI]
            part_s[p, h] = acc[RI:].astype(BF16)
            send(("part", p, h), part_s.at[p, h], part_r.at[p, h], across)

    def share_pre(p):
        for h in range(2):
            recv(("part", p, h), part_r.at[p, h])
            pre[p, h, z, yhi, x] = (own[p, h] + part_r[p, h].astype(F32)).astype(BF16)
            ref = pre.at[p, h, z, yhi, x]
            send(("y", p, h), ref, ref, across)

    def got_pre(p):
        for h in range(2):
            recv(("y", p, h), pre.at[p, h, z, other, x])

    def share_h_out():
        for p in range(SLOTS):
            for zz in range(4):
                send(("ho", p, zz), columns(ho_hbm, p, zz, other, 4 * RO), hob.at[p, zz, pl.ds(RO, RO)], across)

    def share_part_out():
        for p in range(SLOTS):
            for zz in range(4):
                ready(("ho", p, zz))
                recv(("ho", p, zz), hob.at[p, zz, pl.ds(RO, RO)])
        for h in range(2):
            for p in range(SLOTS):
                acc = jnp.zeros((2 * RO, HALF), F32)
                for zz in range(4):
                    acc = acc + dot(hob[p, zz], qog[h, zz, :, p].reshape(4 * RO, HALF))
                owno[h, p] = acc[:RO]
                parto_s[h, p] = acc[RO:].astype(BF16)
            send(("parto", h), parto_s.at[h], parto_r.at[h], across)

    def share_pre_out():
        for h in range(2):
            recv(("parto", h), parto_r.at[h])
            preo[h, z, yhi, x] = (owno[h] + parto_r[h].astype(F32)).astype(BF16)
            ref = preo.at[h, z, yhi, x]
            send(("yo", h), ref, ref, across)

    def got_pre_out():
        for h in range(2):
            recv(("yo", h), preo.at[h, z, other, x])

    def make_left(p):
        for zz in range(4):
            ready(("a", p, zz))
        for h in range(2):
            left[p, h] = dot(acts[p, 0], pre[p, h, 0].reshape(8 * RI, HALF))

            def add(zz, carry):
                left[p, h] += dot(acts[p, zz], pre[p, h, zz].reshape(8 * RI, HALF))
                return carry
            lax.fori_loop(1, 4, add, 0)

    def make_right():
        ready("g")
        for p in range(SLOTS):
            for h in range(2):
                right[p, h] = dot(grads[p], preo[h, :, :, :, p].reshape(DOUT, HALF))

    do("first_pass", q_jobs[0])
    do("first_end", q_jobs[0])
    do("second_send", q_jobs[0])
    share_h_out()
    do("first_pass", q_jobs[1])
    do("first_send", qo_job)
    do("second_pass", q_jobs[0])
    do("first_end", q_jobs[1])
    do("second_send", q_jobs[1])
    do("first_pass", qo_job)
    do("second_end", q_jobs[0])
    share_part(0)
    for zz in range(4):
        share_h(1, zz)
    do("second_pass", q_jobs[1])
    do("first_end", qo_job)
    do("second_send", qo_job)
    share_pre(0)
    do("second_pass", qo_job)
    do("second_end", q_jobs[1])
    got_pre(0)
    do("first_send", p_jobs[0])
    do("second_end", qo_job)
    share_part_out()
    do("first_pass", p_jobs[0])
    share_pre_out()
    do("first_end", p_jobs[0])
    do("second_send", p_jobs[0])
    got_pre_out()
    do("first_send", po_job)
    do("first_pass", po_job)
    share_part(1)
    do("second_pass", p_jobs[0])
    do("first_end", po_job)
    do("second_send", po_job)
    share_pre(1)
    got_pre(1)
    do("first_send", p_jobs[1])
    do("second_pass", po_job)
    do("second_end", p_jobs[0])
    do("first_pass", p_jobs[1])
    do("first_end", p_jobs[1])
    do("second_send", p_jobs[1])
    do("second_end", po_job)
    make_left(0)
    do("second_pass", p_jobs[1])
    make_right()
    do("second_end", p_jobs[1])
    make_left(1)

    r = lax.broadcasted_iota(jnp.int32, (16, HALF), 0)
    c = lax.broadcasted_iota(jnp.int32, (16, HALF), 1)
    first = c // 32 * 2 - c // 128 * 8
    pick = (r // 8 == c // 128) & ((r - r // 8 * 8) * 2 == first)
    pick = jnp.where(pick, 1.0, 0.0).astype(F32)
    for h in range(2):
        product = left[0, h] * right[0, h] + left[1, h] * right[1, h]
        sums = lax.dot_general(
            pick, product, (((1,), (1,)), ((), ())),
            precision=lax.Precision.HIGHEST, preferred_element_type=F32,
        )
        score[pl.ds(2 * h, 2)] = sums.reshape(2, 8, TOK)
    for k, mate in enumerate(mates):
        send(("s", k), score.at[mate[0]], score_r.at[k], mate)
    total = score[group]
    for k in range(3):
        recv(("s", k), score_r.at[k])
        total = total + score_r[k]
    out[...] = total
    for copy in sent:
        copy.wait_send()


def shards(input_acts, output_grads, input_inverse, output_inverse, query_input, query_output, layer_order):
    any_space = pl.BlockSpec(memory_space=pl.ANY)
    result = pl.pallas_call(
        kernel,
        out_shape=jax.ShapeDtypeStruct((8, TOK), F32),
        in_specs=[pl.BlockSpec(memory_space=pltpu.SMEM)] + [any_space] * 6,
        out_specs=pl.BlockSpec(memory_space=pltpu.VMEM),
        scratch_shapes=[
            pltpu.VMEM((8, RI, WIDTH), BF16),
            pltpu.VMEM((8, RO, WIDTH), BF16),
            pltpu.VMEM((SLOTS, 2, 4, 4, RI, HALF), BF16),
            pltpu.VMEM((2, 4, 4, SLOTS, RO, HALF), BF16),
            pltpu.VMEM((SLOTS, 4, 2 * RI, 4 * RI), BF16),
            pltpu.VMEM((SLOTS, 4, 2 * RO, 4 * RO), BF16),
            pltpu.VMEM((SLOTS, 2, RI, HALF), BF16),
            pltpu.VMEM((SLOTS, 2, RI, HALF), BF16),
            pltpu.VMEM((2, SLOTS, RO, HALF), BF16),
            pltpu.VMEM((2, SLOTS, RO, HALF), BF16),
            pltpu.VMEM((SLOTS, 2, RI, HALF), F32),
            pltpu.VMEM((2, SLOTS, RO, HALF), F32),
            pltpu.VMEM((SLOTS, 2, 4, 2, 4, RI, HALF), BF16),
            pltpu.VMEM((2, 4, 2, 4, SLOTS, RO, HALF), BF16),
            pltpu.VMEM((SLOTS, 4, TOK, 8 * RI), BF16),
            pltpu.VMEM((SLOTS, TOK, DOUT), BF16),
            pltpu.VMEM((SLOTS, 2, TOK, HALF), F32),
            pltpu.VMEM((SLOTS, 2, TOK, HALF), F32),
            pltpu.VMEM((4, 8, TOK), F32),
            pltpu.VMEM((3, 8, TOK), F32),
            pltpu.SemaphoreType.DMA((192,)),
            pltpu.SemaphoreType.DMA((192,)),
            pltpu.SemaphoreType.DMA((32,)),
        ],
        compiler_params=pltpu.CompilerParams(
            collective_id=0, has_side_effects=True, vmem_limit_bytes=56 * 2**20
        ),
    )(layer_order, query_input, query_output, input_acts, output_grads, input_inverse, output_inverse)
    return result[:4].T


def solution(mesh):
    in_specs = (
        P("layer", "shard", None),
        P("layer", "shard", None),
        P("layer", "shard", None),
        P("layer", "shard", None),
        P(None, "shard", None),
        P(None, "shard", None),
        P(),
    )
    return jax.shard_map(shards, mesh=mesh, in_specs=in_specs, out_specs=P("shard", "layer"), check_vma=False)
```

time: 327 us -> 135 us (0.41)
  waiting for transfers between devices: 220 us -> 0 us
  Pallas kernels: 0 us -> 133 us
  blocking collectives: 46.7 us -> 0 us
  matrix products: 25.3 us -> 0 us
  between operations: 17.7 us -> 0.01 us
  local copies, waits for them, and re-layouts: 10.3 us -> 1.32 us
  starting transfers between devices: 5.12 us -> 0 us
    all_gather x2 -> x0, waiting for transfers between devices: 186 us -> none  [the longest x1 119 us: shards(): whole_in = lax.all_gather(vectors_in, 'shard', axis=0, tiled=True)]
    pallas_call x0 -> x1, Pallas kernels: none -> 133 us  [shards(): pl.pallas_call(kernel, out_shape=jax.ShapeDtypeStruct((8, TOK), F32), in_...]
    all_to_all x1 -> x0, blocking collectives: 36.1 us -> none  [sent_to_all(): lax.all_to_all(jnp.broadcast_to(shard[None], (devices, *shard.shape)), ax...]
    all_to_all x1 -> x0, waiting for transfers between devices: 34.5 us -> none  [sent_to_all(): lax.all_to_all(jnp.broadcast_to(shard[None], (devices, *shard.shape)), ax...]
    dot_general x4 -> x0, matrix products: 25.3 us -> none  [the longest x1 13.7 us: shards(): jnp.einsum('jti,ijn->jtn', columns, lax.all_gather(folded_in, 'shard', ax...]
    unnamed x1 -> x0, blocking collectives: 10.6 us -> none
    all_to_all x1 -> x0, starting transfers between devices: 5.07 us -> none  [sent_to_all(): lax.all_to_all(jnp.broadcast_to(shard[None], (devices, *shard.shape)), ax...]
    all_to_all x2 -> x0, local copies, waits for them, and re-layouts: 3.4 us -> none  [sent_to_all(): lax.all_to_all(jnp.broadcast_to(shard[None], (devices, *shard.shape)), ax...]
  transfers between devices with their start and end apart: 3 -> 0, of which waited for: 3 -> 0; matrix products, arithmetic and copies ran while one was open for 2% -> 0% of each run, Pallas kernels for 0% -> 0%
where the time goes in v1:
time: 135 us; the launch traced here: 134 us
  Pallas kernels  133 us (99%)
    pallas_call x1, Pallas kernels, shards(): pl.pallas_call(kernel, out_shape=jax.ShapeDtypeStruct((8, TOK), F32), in_...  133 us

profile of v1, /device:TPU:1, one launch (start us, length us, event | category | flops | bytes accessed | tf_op | source)
XLA Modules:
  0.0 134.2 jit_solution(6812208911107474270)
XLA Ops:
  0.0 132.8 %shard_map.73 = f32[8,512]{1,0:T(8,128)} custom-call(s32[8]{0:T(128)} %order.1, bf16[8,160,512]{2,1,0:T(8,128)(2,1)} %q_hbm.1, bf16[8,32,512]{2,1,0:T(8,128)(2,1)} %qo_hbm.1, bf16[2,512,5120]{2,1,0:T(8,128)(2,1)} %a_hbm.1, bf16[2,512,1024]{2,1,0:T(8,128)(2,1)} %g_hbm.1, bf16[2,160,5120]{2,1,0:T(8,128)(2,1)} %h_hbm.1, bf16[2,32,1024]{2,1,0:T(8,128)(2,1)} %ho_hbm.1), custom_call_target="tpu_custom_call" | custom-call | tf_op jit(solution)/shard_map/pallas_call | solution.py:351
  132.9 1.3 slice_bitcast_fusion

commit v2 on v1

v2 whole, which is shorter than its diff:
```python
import functools

import jax
import jax.numpy as jnp
from jax import lax
from jax.experimental import pallas as pl
from jax.experimental.pallas import tpu as pltpu
from jax.sharding import PartitionSpec as P

MESH = pl.DeviceIdType.MESH
BF16 = jnp.bfloat16
F32 = jnp.float32

DIN = 5120
DOUT = 1024
WIDTH = 512
HALF = 256
SLOTS = 2
TOK = 512
RI = 160
RO = 32

SENDS, RECEIVES, LOADS = 34, 96, 8


def dot(a, b):
    return jnp.dot(a, b, preferred_element_type=F32)


def kernel(
    order, q_hbm, qo_hbm, a_hbm, g_hbm, h_hbm, ho_hbm, out,
    q_all, qo_all, qg, qog, hb, hob, part_s, part_r, parto_s, parto_r, own, owno,
    pre, preo, acts, grads, left, right, score, score_r,
    ss, rs, ls,
):
    group = lax.axis_index("layer")
    shard = lax.axis_index("shard")
    ylo, core = lax.div(group, 2), lax.rem(group, 2)
    z, yhi, x = lax.div(shard, 8), lax.rem(lax.div(shard, 4), 2), lax.rem(shard, 4)
    other = 1 - yhi

    def device(zz, yy, xx):
        return (group, zz * 8 + yy * 4 + xx)

    def turn(i, by):
        return lax.rem(i + by + 4, 4)

    near = {
        ("x", 1): device(z, yhi, turn(x, 1)),
        ("x", -1): device(z, yhi, turn(x, -1)),
        ("z", 1): device(turn(z, 1), yhi, x),
        ("z", -1): device(turn(z, -1), yhi, x),
    }
    across = device(z, other, x)
    mates = [
        (ylo * 2 + 1 - core, shard),
        ((1 - ylo) * 2 + core, shard),
        ((1 - ylo) * 2 + 1 - core, shard),
    ]
    sends, receives, loads = {}, {}, {}

    def number(table, name):
        return table.setdefault(name, len(table))

    def send(name, into, src, dst, to):
        pltpu.make_async_remote_copy(
            src_ref=src, dst_ref=dst,
            send_sem=ss.at[number(sends, name)], recv_sem=rs.at[number(receives, into)],
            device_id=to, device_id_type=MESH,
        ).start()

    def wait(name, ref, arrival=True):
        copy = pltpu.make_async_remote_copy(
            src_ref=ref, dst_ref=ref,
            send_sem=ss.at[0 if arrival else number(sends, name)],
            recv_sem=rs.at[number(receives, name) if arrival else 0],
            device_id=across, device_id_type=MESH,
        )
        copy.wait_recv() if arrival else copy.wait_send()

    def left_here(name, ref):
        wait(name, ref, arrival=False)

    def fetch(name, src, dst):
        pltpu.make_async_copy(src, dst, ls.at[number(loads, name)]).start()

    def ready(name, ref):
        pltpu.make_async_copy(ref, ref, ls.at[number(loads, name)]).wait()

    class Gather:
        def __init__(self, name, first, at, half):
            self.name, self.at, self.half = name, at, half
            self.first, self.second = first, "z" if first == "x" else "x"
            self.i, self.j = (x, z) if first == "x" else (z, x)

        def place(self, i, j):
            return self.at(j, i) if self.first == "x" else self.at(i, j)

        def block(self, i, part):
            return self.half(self.place(i, self.j), part)

        def line(self, j, part):
            return self.place(pl.ds(2 * part, 2), j)

        def key(self, k):
            return (self.name, k)

        def first_send(self):
            for by, parts in ((1, (0, 1)), (-1, (1, 0))):
                for k, part in enumerate(parts):
                    ref = self.block(self.i, part)
                    send(self.key("f"), self.key("f" if k else by), ref, ref, near[self.first, by])

        def first_pass(self):
            for by, part in ((1, 0), (-1, 1)):
                ref = self.block(turn(self.i, -by), part)
                wait(self.key(by), ref)
                send(self.key("f"), self.key("f"), ref, ref, near[self.first, by])

        def first_end(self):
            wait(self.key("f"), self.place(pl.ds(0, 2), self.j))

        def second_send(self):
            for by, parts in ((1, (0, 1)), (-1, (1, 0))):
                for k, part in enumerate(parts):
                    ref = self.line(self.j, part)
                    send(self.key("s"), self.key("near" if k else 2 * by), ref, ref, near[self.second, by])

        def second_pass(self):
            for by, part in ((1, 0), (-1, 1)):
                ref = self.line(turn(self.j, -by), part)
                wait(self.key(2 * by), ref)
                send(self.key("s"), self.key("far"), ref, ref, near[self.second, by])

        def second_near(self):
            wait(self.key("near"), self.place(pl.ds(0, 4), self.j))

        def second_far(self):
            wait(self.key("far"), self.place(pl.ds(0, 4), self.j))

        def second_end(self):
            self.second_near()
            self.second_far()

        def finish(self):
            left_here(self.key("f"), self.place(pl.ds(0, 3), self.j))
            left_here(self.key("s"), self.place(pl.ds(0, 4), pl.ds(0, 3)))

    rows = lambda ref, part: ref.at[..., pl.ds(RI // 2 * part, RI // 2), :]
    slots = lambda ref, part: ref.at[..., pl.ds(part, 1), :, :]
    axes = ("x", "z")

    def pair(make):
        return [make(h) for h in range(2)]

    def q_job(p):
        return pair(lambda h: Gather(("q", p, h), axes[h], lambda zz, xx: qg.at[p, h, zz, xx], rows))

    def p_job(p):
        return pair(lambda h: Gather(("p", p, h), axes[h], lambda zz, xx: pre.at[p, h, zz, :, xx], rows))

    qo_job = pair(lambda h: Gather(("qo", h), axes[h], lambda zz, xx: qog.at[h, zz, xx], slots))
    po_job = pair(lambda h: Gather(("po", h), axes[h], lambda zz, xx: preo.at[h, zz, yhi, xx], slots))
    q_jobs, p_jobs = [q_job(0), q_job(1)], [p_job(0), p_job(1)]

    def do(step, job):
        for gather in job:
            getattr(gather, step)()

    def columns(ref, p, zz, yy, width):
        return ref.at[p, :, pl.ds(pl.multiple_of((zz * 2 + yy) * width, width), width)]

    fetch("qo", qo_hbm, qo_all)
    fetch("q", q_hbm, q_all)
    barrier = pltpu.get_barrier_semaphore()
    peers = list(near.values()) + [across] + mates
    for peer in peers:
        pl.semaphore_signal(barrier, inc=1, device_id=peer, device_id_type=MESH)
    h_own = [hb.at[p, :, pl.ds(0, RI)] for p in range(SLOTS)]
    h_other = [hb.at[p, :, pl.ds(RI, RI)] for p in range(SLOTS)]
    ho_own, ho_other = hob.at[:, :, pl.ds(0, RO)], hob.at[:, :, pl.ds(RO, RO)]
    for p in range(SLOTS):
        for zz in range(4):
            fetch("ho", columns(ho_hbm, p, zz, yhi, 4 * RO), ho_own.at[p, zz])
    for p in range(SLOTS):
        for zz in range(4):
            fetch(("h", p), columns(h_hbm, p, zz, yhi, 4 * RI), h_own[p].at[zz])

    def share_h(p):
        for zz in range(4):
            send(("h", p), ("h", p), columns(h_hbm, p, zz, other, 4 * RI), h_other[p].at[zz], across)

    def share_h_out():
        for p in range(SLOTS):
            for zz in range(4):
                send("ho", "ho", columns(ho_hbm, p, zz, other, 4 * RO), ho_other.at[p, zz], across)

    def share_part(p):
        ready(("h", p), h_own[p])
        wait(("h", p), h_other[p])
        for h in range(2):
            def add(zz, acc):
                return acc + dot(hb[p, zz], qg[p, h, zz].reshape(4 * RI, HALF))
            acc = lax.fori_loop(0, 4, add, jnp.zeros((2 * RI, HALF), F32))
            own[p, h] = acc[:RI]
            part_s[p, h] = acc[RI:].astype(BF16)
            send(("part", p), ("part", p, h), part_s.at[p, h], part_r.at[p, h], across)

    def share_pre(p):
        for h in range(2):
            wait(("part", p, h), part_r.at[p, h])
            pre[p, h, z, yhi, x] = (own[p, h] + part_r[p, h].astype(F32)).astype(BF16)
            ref = pre.at[p, h, z, yhi, x]
            send(("y", p), ("y", p), ref, ref, across)

    def got_pre(p):
        wait(("y", p), pre.at[p, :, z, other, x])

    def share_part_out():
        ready("ho", ho_own)
        wait("ho", ho_other)
        for h in range(2):
            for p in range(SLOTS):
                acc = jnp.zeros((2 * RO, HALF), F32)
                for zz in range(4):
                    acc = acc + dot(hob[p, zz], qog[h, zz, :, p].reshape(4 * RO, HALF))
                owno[h, p] = acc[:RO]
                parto_s[h, p] = acc[RO:].astype(BF16)
        send("parto", "parto", parto_s, parto_r, across)

    def make_pre_out():
        wait("parto", parto_r)
        for h in range(2):
            preo[h, z, yhi, x] = (owno[h] + parto_r[h].astype(F32)).astype(BF16)

    def share_pre_out():
        for h in range(2):
            ref = preo.at[h, :, yhi]
            send("yo", "yo", ref, ref, across)

    def add_left(p, h, zz):
        left[p, h] += dot(acts[p, zz], pre[p, h, zz].reshape(8 * RI, HALF))

    def start_left(p, h):
        left[p, h] = dot(acts[p, z], pre[p, h, z].reshape(8 * RI, HALF))

    def near_left(p, h):
        def add(k, carry):
            add_left(p, h, turn(z, 2 * k - 1))
            return carry
        lax.fori_loop(0, 2, add, 0)

    def far_left(p, h):
        add_left(p, h, turn(z, 2))

    def make_left(p, h):
        start_left(p, h)
        near_left(p, h)
        far_left(p, h)

    def got_acts(p):
        ready(("a", p), acts.at[p])

    def make_right():
        ready("g", grads)
        wait("yo", preo.at[:, :, other])
        for p in range(SLOTS):
            for h in range(2):
                right[p, h] = dot(grads[p], preo[h, :, :, :, p].reshape(DOUT, HALF))

    def place_q(p):
        m = order[group * SLOTS + p]
        for h in range(2):
            qg[p, h, z, x] = q_all[m, :, pl.ds(h * HALF, HALF)]

    def place_q_out():
        for p in range(SLOTS):
            m = order[group * SLOTS + p]
            for h in range(2):
                qog[h, z, x, p] = qo_all[m, :, pl.ds(h * HALF, HALF)]

    def load_rest():
        for p in range(SLOTS):
            for zz in range(4):
                fetch(("a", p), a_hbm.at[p, :, pl.ds(zz * 8 * RI, 8 * RI)], acts.at[p, zz])
        fetch("g", g_hbm, grads)

    schedule = [
        (pl.semaphore_wait, barrier, len(peers)),
        (share_h_out,),
        (share_h, 0),
        (ready, "qo", qo_all),
        (place_q_out,),
        (do, "first_send", qo_job),
        (ready, "q", q_all),
        (place_q, 0),
        (do, "first_send", q_jobs[0]),
        (place_q, 1),
        (do, "first_pass", qo_job),
        (do, "first_send", q_jobs[1]),
        (load_rest,),
        (do, "first_end", qo_job),
        (do, "second_send", qo_job),
        (do, "first_pass", q_jobs[0]),
        (do, "second_pass", qo_job),
        (do, "first_end", q_jobs[0]),
        (do, "second_send", q_jobs[0]),
        (do, "first_pass", q_jobs[1]),
        (do, "second_end", qo_job),
        (share_part_out,),
        (do, "first_end", q_jobs[1]),
        (do, "second_pass", q_jobs[0]),
        (do, "second_send", q_jobs[1]),
        (make_pre_out,),
        (do, "first_send", po_job),
        (do, "second_end", q_jobs[0]),
        (share_part, 0),
        (do, "first_pass", po_job),
        (do, "second_pass", q_jobs[1]),
        (do, "first_end", po_job),
        (do, "second_send", po_job),
        (share_pre, 0),
        (share_h, 1),
        (do, "second_pass", po_job),
        (got_pre, 0),
        (do, "first_send", p_jobs[0]),
        (do, "second_end", q_jobs[1]),
        (do, "second_end", po_job),
        (do, "first_pass", p_jobs[0]),
        (do, "first_end", p_jobs[0]),
        (do, "second_send", p_jobs[0]),
        (got_acts, 0),
        (got_acts, 1),
        (do, "second_pass", p_jobs[0]),
        (share_part, 1),
        (share_pre, 1),
        (share_pre_out,),
        (got_pre, 1),
        (do, "first_send", p_jobs[1]),
        (do, "second_end", p_jobs[0]),
        (do, "first_pass", p_jobs[1]),
        (do, "first_end", p_jobs[1]),
        (do, "second_send", p_jobs[1]),
        (make_left, 0, 0),
        (make_left, 0, 1),
        (do, "second_pass", p_jobs[1]),
        (start_left, 1, 0),
        (do, "second_near", p_jobs[1]),
        (near_left, 1, 0),
        (make_right,),
        (do, "second_far", p_jobs[1]),
        (far_left, 1, 0),
        (make_left, 1, 1),
    ]
    for step, *given in schedule:
        step(*given)

    r = lax.broadcasted_iota(jnp.int32, (16, HALF), 0)
    c = lax.broadcasted_iota(jnp.int32, (16, HALF), 1)
    first = c // 32 * 2 - c // 128 * 8
    pick = (r // 8 == c // 128) & ((r - r // 8 * 8) * 2 == first)
    pick = jnp.where(pick, 1.0, 0.0).astype(F32)
    for h in range(2):
        product = left[0, h] * right[0, h] + left[1, h] * right[1, h]
        sums = lax.dot_general(
            pick, product, (((1,), (1,)), ((), ())),
            precision=lax.Precision.HIGHEST, preferred_element_type=F32,
        )
        score[pl.ds(2 * h, 2)] = sums.reshape(2, 8, TOK)
    for k, mate in enumerate(mates):
        send("score", "score", score.at[mate[0]], score_r.at[k], mate)
    wait("score", score_r)
    out[...] = (score[group] + score_r[0]) + (score_r[1] + score_r[2])

    for job in [qo_job, po_job] + q_jobs + p_jobs:
        do("finish", job)
    for p in range(SLOTS):
        left_here(("h", p), h_other[p])
        left_here(("part", p), part_s.at[p])
        left_here(("y", p), pre.at[p, :, z, yhi, x])
    left_here("ho", ho_other)
    left_here("parto", parto_s)
    left_here("yo", preo.at[:, :, yhi])
    left_here("score", score_r)
    assert (len(sends), len(receives), len(loads)) == (SENDS, RECEIVES, LOADS)


def shards(input_acts, output_grads, input_inverse, output_inverse, query_input, query_output, layer_order):
    any_space = pl.BlockSpec(memory_space=pl.ANY)
    result = pl.pallas_call(
        kernel,
        out_shape=jax.ShapeDtypeStruct((8, TOK), F32),
        in_specs=[pl.BlockSpec(memory_space=pltpu.SMEM)] + [any_space] * 6,
        out_specs=pl.BlockSpec(memory_space=pltpu.VMEM),
        scratch_shapes=[
            pltpu.VMEM((8, RI, WIDTH), BF16),
            pltpu.VMEM((8, RO, WIDTH), BF16),
            pltpu.VMEM((SLOTS, 2, 4, 4, RI, HALF), BF16),
            pltpu.VMEM((2, 4, 4, SLOTS, RO, HALF), BF16),
            pltpu.VMEM((SLOTS, 4, 2 * RI, 4 * RI), BF16),
            pltpu.VMEM((SLOTS, 4, 2 * RO, 4 * RO), BF16),
            pltpu.VMEM((SLOTS, 2, RI, HALF), BF16),
            pltpu.VMEM((SLOTS, 2, RI, HALF), BF16),
            pltpu.VMEM((2, SLOTS, RO, HALF), BF16),
            pltpu.VMEM((2, SLOTS, RO, HALF), BF16),
            pltpu.VMEM((SLOTS, 2, RI, HALF), F32),
            pltpu.VMEM((2, SLOTS, RO, HALF), F32),
            pltpu.VMEM((SLOTS, 2, 4, 2, 4, RI, HALF), BF16),
            pltpu.VMEM((2, 4, 2, 4, SLOTS, RO, HALF), BF16),
            pltpu.VMEM((SLOTS, 4, TOK, 8 * RI), BF16),
            pltpu.VMEM((SLOTS, TOK, DOUT), BF16),
            pltpu.VMEM((SLOTS, 2, TOK, HALF), F32),
            pltpu.VMEM((SLOTS, 2, TOK, HALF), F32),
            pltpu.VMEM((4, 8, TOK), F32),
            pltpu.VMEM((3, 8, TOK), F32),
            pltpu.SemaphoreType.DMA((SENDS,)),
            pltpu.SemaphoreType.DMA((RECEIVES,)),
            pltpu.SemaphoreType.DMA((LOADS,)),
        ],
        compiler_params=pltpu.CompilerParams(
            collective_id=0, has_side_effects=True, vmem_limit_bytes=56 * 2**20
        ),
    )(layer_order, query_input, query_output, input_acts, output_grads, input_inverse, output_inverse)
    return result[:4].T


def solution(mesh):
    in_specs = (
        P("layer", "shard", None),
        P("layer", "shard", None),
        P("layer", "shard", None),
        P("layer", "shard", None),
        P(None, "shard", None),
        P(None, "shard", None),
        P(),
    )
    return jax.shard_map(shards, mesh=mesh, in_specs=in_specs, out_specs=P("shard", "layer"), check_vma=False)
```

time: 135 us -> 117 us (0.87)
  Pallas kernels: 133 us -> 116 us
    pallas_call x1, Pallas kernels: 133 us -> 116 us  [shards(): pl.pallas_call(kernel, out_shape=jax.ShapeDtypeStruct((8, TOK), F32), in_...]
where the time goes in v2:
time: 117 us
  Pallas kernels  116 us (99%)
  local copies, waits for them, and re-layouts  1.32 us (1%)
    pallas_call x1, Pallas kernels, shards(): pl.pallas_call(kernel, out_shape=jax.ShapeDtypeStruct((8, TOK), F32), in_...  116 us

profile of v2, /device:TPU:1, one launch (start us, length us, event | category | flops | bytes accessed | tf_op | source)
XLA Modules:
  0.0 117.2 jit_solution(6237730845256178972)
XLA Ops:
  0.0 115.9 %shard_map.73 = f32[8,512]{1,0:T(8,128)} custom-call(s32[8]{0:T(128)} %order.1, bf16[8,160,512]{2,1,0:T(8,128)(2,1)} %q_hbm.1, bf16[8,32,512]{2,1,0:T(8,128)(2,1)} %qo_hbm.1, bf16[2,512,5120]{2,1,0:T(8,128)(2,1)} %a_hbm.1, bf16[2,512,1024]{2,1,0:T(8,128)(2,1)} %g_hbm.1, bf16[2,160,5120]{2,1,0:T(8,128)(2,1)} %h_hbm.1, bf16[2,32,1024]{2,1,0:T(8,128)(2,1)} %ho_hbm.1), custom_call_target="tpu_custom_call" | custom-call | tf_op jit(solution)/shard_map/pallas_call | solution.py:390
  115.9 1.3 %slice_bitcast_fusion = f32[512,4]{0,1:T(4,128)} fusion(f32[8,512]{1,0:T(8,128)} %shard_map.73), kind=kLoop, calls=%fused_computation | loop fusion | bytes 16384 | tf_op jit(solution)/shard_map/transpose | solution.py:424

commit v3 on v2

--- a/solution.py
+++ b/solution.py
@@ -20,7 +20,7 @@
 RI = 160
 RO = 32
 
-SENDS, RECEIVES, LOADS = 34, 96, 8
+SENDS, RECEIVES, LOADS = 42, 100, 8
 
 
 def dot(a, b):
@@ -96,51 +96,86 @@
         def place(self, i, j):
             return self.at(j, i) if self.first == "x" else self.at(i, j)
 
-        def block(self, i, part):
-            return self.half(self.place(i, self.j), part)
-
-        def line(self, j, part):
-            return self.place(pl.ds(2 * part, 2), j)
-
         def key(self, k):
             return (self.name, k)
+
+        def pass_on(self, axis, by, count, into, ref):
+            send(self.key(count), self.key(into), ref, ref, near[axis, by])
+
+        def s0(self):
+            ref = self.place(self.i, self.j)
+            for by in (1, -1):
+                self.pass_on(self.first, by, "f", "a", ref)
+            for by in (1, -1):
+                self.pass_on(self.second, by, "s", "c0", ref)
+
+        def s1(self):
+            wait(self.key("a"), self.place(pl.ds(0, 2), self.j))
+            for by, part in ((1, 0), (-1, 1)):
+                ref = self.half(self.place(turn(self.i, -by), self.j), part)
+                self.pass_on(self.first, by, "f", "b", ref)
+            for off in (1, -1):
+                ref = self.place(turn(self.i, off), self.j)
+                for by in (1, -1):
+                    self.pass_on(self.second, by, "s", "c1", ref)
+
+        def s2(self):
+            wait(self.key("b"), self.place(self.i, self.j))
+            ref = self.place(turn(self.i, 2), self.j)
+            for by in (1, -1):
+                self.pass_on(self.second, by, "s", "c2", ref)
+
+        def forward(self, i):
+            for by, part in ((1, 0), (-1, 1)):
+                ref = self.half(self.place(i, turn(self.j, -by)), part)
+                self.pass_on(self.second, by, "s", "d", ref)
+
+        def s3(self):
+            wait(self.key("c0"), self.place(pl.ds(0, 2), self.j))
+            self.forward(self.i)
+
+        def s4(self):
+            wait(self.key("c1"), self.place(pl.ds(0, 4), self.j))
+            self.forward(turn(self.i, 1))
+            self.forward(turn(self.i, -1))
+
+        def s5(self):
+            wait(self.key("c2"), self.place(pl.ds(0, 2), self.j))
+            self.forward(turn(self.i, 2))
+
+        def end(self):
+            wait(self.key("d"), self.place(pl.ds(0, 4), self.j))
 
         def first_send(self):
             for by, parts in ((1, (0, 1)), (-1, (1, 0))):
                 for k, part in enumerate(parts):
-                    ref = self.block(self.i, part)
-                    send(self.key("f"), self.key("f" if k else by), ref, ref, near[self.first, by])
+                    ref = self.half(self.place(self.i, self.j), part)
+                    self.pass_on(self.first, by, "f", "b" if k else "a", ref)
 
         def first_pass(self):
+            wait(self.key("a"), self.place(self.i, self.j))
             for by, part in ((1, 0), (-1, 1)):
-                ref = self.block(turn(self.i, -by), part)
-                wait(self.key(by), ref)
-                send(self.key("f"), self.key("f"), ref, ref, near[self.first, by])
+                ref = self.half(self.place(turn(self.i, -by), self.j), part)
+                self.pass_on(self.first, by, "f", "b", ref)
 
         def first_end(self):
-            wait(self.key("f"), self.place(pl.ds(0, 2), self.j))
+            wait(self.key("b"), self.place(pl.ds(0, 2), self.j))
 
         def second_send(self):
             for by, parts in ((1, (0, 1)), (-1, (1, 0))):
                 for k, part in enumerate(parts):
-                    ref = self.line(self.j, part)
-                    send(self.key("s"), self.key("near" if k else 2 * by), ref, ref, near[self.second, by])
+                    ref = self.place(pl.ds(2 * part, 2), self.j)
+                    self.pass_on(self.second, by, "s", "c1" if k else "c0", ref)
 
         def second_pass(self):
+            wait(self.key("c0"), self.place(pl.ds(0, 4), self.j))
             for by, part in ((1, 0), (-1, 1)):
-                ref = self.line(turn(self.j, -by), part)
-                wait(self.key(2 * by), ref)
-                send(self.key("s"), self.key("far"), ref, ref, near[self.second, by])
-
-        def second_near(self):
-            wait(self.key("near"), self.place(pl.ds(0, 4), self.j))
-
-        def second_far(self):
-            wait(self.key("far"), self.place(pl.ds(0, 4), self.j))
+                ref = self.place(pl.ds(2 * part, 2), turn(self.j, -by))
+                self.pass_on(self.second, by, "s", "d", ref)
 
         def second_end(self):
-            self.second_near()
-            self.second_far()
+            wait(self.key("c1"), self.place(pl.ds(0, 4), self.j))
+            wait(self.key("d"), self.place(pl.ds(0, 4), self.j))
 
         def finish(self):
             left_here(self.key("f"), self.place(pl.ds(0, 3), self.j))
@@ -156,12 +191,14 @@
     def q_job(p):
         return pair(lambda h: Gather(("q", p, h), axes[h], lambda zz, xx: qg.at[p, h, zz, xx], rows))
 
-    def p_job(p):
-        return pair(lambda h: Gather(("p", p, h), axes[h], lambda zz, xx: pre.at[p, h, zz, :, xx], rows))
+    def p_job(p, k):
+        yy = (yhi, other)[k]
+        return pair(lambda h: Gather(("p", p, k, h), axes[h], lambda zz, xx: pre.at[p, h, zz, yy, xx], rows))
 
     qo_job = pair(lambda h: Gather(("qo", h), axes[h], lambda zz, xx: qog.at[h, zz, xx], slots))
     po_job = pair(lambda h: Gather(("po", h), axes[h], lambda zz, xx: preo.at[h, zz, yhi, xx], slots))
-    q_jobs, p_jobs = [q_job(0), q_job(1)], [p_job(0), p_job(1)]
+    q0_job, q1_job = q_job(0), q_job(1)
+    p0_job, p1_job, p0_far, p1_far = p_job(0, 0), p_job(1, 0), p_job(0, 1), p_job(1, 1)
 
     def do(step, job):
         for gather in job:
@@ -186,8 +223,8 @@
         for zz in range(4):
             fetch(("h", p), columns(h_hbm, p, zz, yhi, 4 * RI), h_own[p].at[zz])
 
-    def share_h(p):
-        for zz in range(4):
+    def share_h(p, *some):
+        for zz in some or range(4):
             send(("h", p), ("h", p), columns(h_hbm, p, zz, other, 4 * RI), h_other[p].at[zz], across)
 
     def share_h_out():
@@ -238,25 +275,19 @@
             ref = preo.at[h, :, yhi]
             send("yo", "yo", ref, ref, across)
 
-    def add_left(p, h, zz):
-        left[p, h] += dot(acts[p, zz], pre[p, h, zz].reshape(8 * RI, HALF))
-
-    def start_left(p, h):
-        left[p, h] = dot(acts[p, z], pre[p, h, z].reshape(8 * RI, HALF))
-
-    def near_left(p, h):
-        def add(k, carry):
-            add_left(p, h, turn(z, 2 * k - 1))
-            return carry
-        lax.fori_loop(0, 2, add, 0)
-
-    def far_left(p, h):
-        add_left(p, h, turn(z, 2))
-
-    def make_left(p, h):
-        start_left(p, h)
-        near_left(p, h)
-        far_left(p, h)
+    def make_left(p, yy, fresh):
+        k = pl.ds(pl.multiple_of(yy * 4 * RI, 4 * RI), 4 * RI)
+        for h in range(2):
+            def part(zz):
+                return dot(acts[p, zz, :, k], pre[p, h, zz, yy].reshape(4 * RI, HALF))
+
+            def add(zz, carry):
+                left[p, h] += part(zz)
+                return carry
+
+            if fresh:
+                left[p, h] = part(0)
+            lax.fori_loop(1 if fresh else 0, 4, add, 0)
 
     def got_acts(p):
         ready(("a", p), acts.at[p])
@@ -289,68 +320,84 @@
         (pl.semaphore_wait, barrier, len(peers)),
         (share_h_out,),
         (share_h, 0),
+        (share_h, 1, 0),
         (ready, "qo", qo_all),
         (place_q_out,),
-        (do, "first_send", qo_job),
+        (do, "s0", qo_job),
         (ready, "q", q_all),
         (place_q, 0),
-        (do, "first_send", q_jobs[0]),
+        (do, "first_send", q0_job),
         (place_q, 1),
-        (do, "first_pass", qo_job),
-        (do, "first_send", q_jobs[1]),
+        (do, "s3", qo_job),
+        (do, "s1", qo_job),
+        (do, "first_pass", q0_job),
+        (do, "first_send", q1_job),
         (load_rest,),
-        (do, "first_end", qo_job),
-        (do, "second_send", qo_job),
-        (do, "first_pass", q_jobs[0]),
-        (do, "second_pass", qo_job),
-        (do, "first_end", q_jobs[0]),
-        (do, "second_send", q_jobs[0]),
-        (do, "first_pass", q_jobs[1]),
-        (do, "second_end", qo_job),
+        (do, "s2", qo_job),
+        (do, "s4", qo_job),
+        (do, "first_end", q0_job),
+        (do, "second_send", q0_job),
+        (do, "first_pass", q1_job),
+        (do, "s5", qo_job),
+        (do, "second_pass", q0_job),
+        (do, "first_end", q1_job),
+        (do, "second_send", q1_job),
+        (do, "end", qo_job),
         (share_part_out,),
-        (do, "first_end", q_jobs[1]),
-        (do, "second_pass", q_jobs[0]),
-        (do, "second_send", q_jobs[1]),
+        (do, "second_end", q0_job),
+        (share_part, 0),
         (make_pre_out,),
-        (do, "first_send", po_job),
-        (do, "second_end", q_jobs[0]),
-        (share_part, 0),
-        (do, "first_pass", po_job),
-        (do, "second_pass", q_jobs[1]),
-        (do, "first_end", po_job),
-        (do, "second_send", po_job),
+        (do, "s0", po_job),
+        (do, "second_pass", q1_job),
         (share_pre, 0),
-        (share_h, 1),
-        (do, "second_pass", po_job),
+        (share_h, 1, 1),
+        (share_h, 1, 2),
+        (share_h, 1, 3),
+        (do, "first_send", p0_job),
+        (do, "s1", po_job),
+        (do, "s3", po_job),
+        (do, "second_end", q1_job),
+        (do, "first_pass", p0_job),
         (got_pre, 0),
-        (do, "first_send", p_jobs[0]),
-        (do, "second_end", q_jobs[1]),
-        (do, "second_end", po_job),
-        (do, "first_pass", p_jobs[0]),
-        (do, "first_end", p_jobs[0]),
-        (do, "second_send", p_jobs[0]),
+        (do, "s0", p0_far),
+        (do, "s2", po_job),
+        (do, "s4", po_job),
+        (do, "first_end", p0_job),
+        (do, "second_send", p0_job),
+        (do, "s1", p0_far),
+        (do, "s5", po_job),
+        (do, "s3", p0_far),
+        (do, "second_pass", p0_job),
+        (share_part, 1),
+        (share_pre, 1),
+        (do, "s0", p1_job),
+        (do, "end", po_job),
+        (do, "s2", p0_far),
+        (do, "s4", p0_far),
+        (share_pre_out,),
+        (do, "second_end", p0_job),
         (got_acts, 0),
         (got_acts, 1),
-        (do, "second_pass", p_jobs[0]),
-        (share_part, 1),
-        (share_pre, 1),
-        (share_pre_out,),
+        (make_left, 0, yhi, True),
         (got_pre, 1),
-        (do, "first_send", p_jobs[1]),
-        (do, "second_end", p_jobs[0]),
-        (do, "first_pass", p_jobs[1]),
-        (do, "first_end", p_jobs[1]),
-        (do, "second_send", p_jobs[1]),
-        (make_left, 0, 0),
-        (make_left, 0, 1),
-        (do, "second_pass", p_jobs[1]),
-        (start_left, 1, 0),
-        (do, "second_near", p_jobs[1]),
-        (near_left, 1, 0),
+        (do, "first_send", p1_far),
+        (do, "s1", p1_job),
+        (do, "s3", p1_job),
+        (do, "s5", p0_far),
+        (do, "first_pass", p1_far),
+        (do, "s2", p1_job),
+        (do, "s4", p1_job),
+        (do, "end", p0_far),
+        (make_left, 0, other, False),
+        (do, "first_end", p1_far),
+        (do, "second_send", p1_far),
+        (do, "s5", p1_job),
         (make_right,),
-        (do, "second_far", p_jobs[1]),
-        (far_left, 1, 0),
-        (make_left, 1, 1),
+        (do, "second_pass", p1_far),
+        (do, "end", p1_job),
+        (make_left, 1, yhi, True),
+        (do, "second_end", p1_far),
+        (make_left, 1, other, False),
     ]
     for step, *given in schedule:
         step(*given)
@@ -372,7 +419,7 @@
     wait("score", score_r)
     out[...] = (score[group] + score_r[0]) + (score_r[1] + score_r[2])
 
-    for job in [qo_job, po_job] + q_jobs + p_jobs:
+    for job in [qo_job, po_job, q0_job, q1_job, p0_job, p1_job, p0_far, p1_far]:
         do("finish", job)
     for p in range(SLOTS):
         left_here(("h", p), h_other[p])
@@ -382,7 +429,7 @@
     left_here("parto", parto_s)
     left_here("yo", preo.at[:, :, yhi])
     left_here("score", score_r)
-    assert (len(sends), len(receives), len(loads)) == (SENDS, RECEIVES, LOADS)
+    assert (len(sends), len(receives), len(loads)) == (SENDS, RECEIVES, LOADS), len(receives)
 
 
 def shards(input_acts, output_grads, input_inverse, output_inverse, query_input, query_output, layer_order):

time: 117 us -> 112 us (0.957)
  Pallas kernels: 116 us -> 111 us
    pallas_call x1, Pallas kernels: 116 us -> 111 us  [shards(): pl.pallas_call(kernel, out_shape=jax.ShapeDtypeStruct((8, TOK), F32), in_...]
where the time goes in v3:
time: 112 us
  Pallas kernels  111 us (99%)
  local copies, waits for them, and re-layouts  1.32 us (1%)
    pallas_call x1, Pallas kernels, shards(): pl.pallas_call(kernel, out_shape=jax.ShapeDtypeStruct((8, TOK), F32), in_...  111 us

profile of v3, /device:TPU:1, one launch (start us, length us, event | category | flops | bytes accessed | tf_op | source)
XLA Modules:
  0.0 112.2 jit_solution(9591858450549240852)
XLA Ops:
  0.0 110.8 %shard_map.73 = f32[8,512]{1,0:T(8,128)} custom-call(s32[8]{0:T(128)} %order.1, bf16[8,160,512]{2,1,0:T(8,128)(2,1)} %q_hbm.1, bf16[8,32,512]{2,1,0:T(8,128)(2,1)} %qo_hbm.1, bf16[2,512,5120]{2,1,0:T(8,128)(2,1)} %a_hbm.1, bf16[2,512,1024]{2,1,0:T(8,128)(2,1)} %g_hbm.1, bf16[2,160,5120]{2,1,0:T(8,128)(2,1)} %h_hbm.1, bf16[2,32,1024]{2,1,0:T(8,128)(2,1)} %ho_hbm.1), custom_call_target="tpu_custom_call" | custom-call | tf_op jit(solution)/shard_map/pallas_call | solution.py:437
  110.9 1.3 %slice_bitcast_fusion = f32[512,4]{0,1:T(4,128)} fusion(f32[8,512]{1,0:T(8,128)} %shard_map.73), kind=kLoop, calls=%fused_computation | loop fusion | bytes 16384 | tf_op jit(solution)/shard_map/transpose | solution.py:471
